TPU v7x, 128 devices: a whole 4x4x4 slice. The times are simulated.
128 devices in a mesh: dp: 16 (over z, x), seq: 8 (over y, core).
Axes of the slice: x: 4, y: 4, z: 4, core: 2. Of those that a mesh axis runs over, the one named last changes fastest.
Arguments:
- layer_input: bfloat16 [2, 16, 1024, 896], P(None, 'dp', 'seq'), may hold values from -6 to 6
- pic_start: int32 [2, 16], P(None, 'dp'), may hold values from 0 to 768, as said below
- norm_one: bfloat16 [896], P('dp'), may hold values from 0.099609375 to 1.8984375
- w_query: bfloat16 [896, 896], P('dp'), may hold values from -0.1875 to 0.1875
- b_query: bfloat16 [896], P('dp'), may hold values from -3 to 3
- w_key: bfloat16 [896, 128], P('dp'), may hold values from -0.1875 to 0.1875
- b_key: bfloat16 [128], P('dp'), may hold values from -3 to 3
- w_value: bfloat16 [896, 128], P('dp'), may hold values from -0.1875 to 0.1875
- b_value: bfloat16 [128], P('dp'), may hold values from -3 to 3
- w_out: bfloat16 [896, 896], P('dp'), may hold values from -1.5 to 1.5
- norm_two: bfloat16 [896], P('dp'), may hold values from 0.099609375 to 1.8984375
- w_gate: bfloat16 [896, 4864], P('dp'), may hold values from -0.1875 to 0.1875
- w_up: bfloat16 [896, 4864], P('dp'), may hold values from -0.1875 to 0.1875
- w_down: bfloat16 [4864, 896], P('dp'), may hold values from -0.078125 to 0.078125
- out_grad: bfloat16 [2, 16, 1024, 896], P(None, 'dp', 'seq'), may hold values from -6 to 6
Outputs:
- layer_output: bfloat16 [2, 16, 1024, 896], P(None, 'dp', 'seq')
- input_grad: float32 [2, 16, 1024, 896], P(None, 'dp', 'seq')
- norm_one_grad: float32 [896], P('dp')
- w_query_grad: float32 [896, 896], P('dp')
- b_query_grad: float32 [896], P('dp')
- w_key_grad: float32 [896, 128], P('dp')
- b_key_grad: float32 [128], P('dp')
- w_value_grad: float32 [896, 128], P('dp')
- b_value_grad: float32 [128], P('dp')
- w_out_grad: float32 [896, 896], P('dp')
- norm_two_grad: float32 [896], P('dp')
- w_gate_grad: float32 [896, 4864], P('dp')
- w_up_grad: float32 [896, 4864], P('dp')
- w_down_grad: float32 [4864, 896], P('dp')
Inputs may be any that keep to these rules, and one draw needn't show every extreme that they name: Each sequence has one picture block of 256 tokens starting at its pic_start, a multiple of 256.
All inputs are finite; a program needn't handle non-finite values.
Results may differ from a plain program's by a relative error of at most 0.028.
Values may be sent and summed in bfloat16 or wider, within the bound.
A program may use at most 192 MiB of HBM per device.

v0:
```python
import jax
import jax.numpy as jnp
from jax import lax
from jax.sharding import PartitionSpec as P

HEADS = 14
KV_HEADS = 2
HD = 64
PIC = 256


EPSILON = 1e-06
ROPE_BASE = 1000000.0
NEGATIVE = -1e30


def rope_tables(positions, head_dim):
    half_dim = head_dim // 2
    exponent = jnp.arange(half_dim, dtype=jnp.float32) * (2.0 / head_dim)
    inverse = ROPE_BASE ** (-exponent)
    angles = positions.astype(jnp.float32)[:, None] * inverse[None, :]
    angles = jnp.concatenate([angles, angles], axis=1)
    return (jnp.cos(angles), jnp.sin(angles))


def rotate_half(inputs, head_dim):
    shaped = inputs.reshape(inputs.shape[:-1] + (inputs.shape[-1] // head_dim, 2, head_dim // 2))
    turned = jnp.stack([-shaped[..., 1, :], shaped[..., 0, :]], axis=-2)
    return turned.reshape(inputs.shape)


def rotate(inputs, cosine, sine, head_dim, direction):
    count = inputs.shape[-1] // head_dim
    cos_all = jnp.tile(cosine, (1, count))
    sin_all = jnp.tile(sine, (1, count))
    return inputs * cos_all + direction * rotate_half(inputs, head_dim) * sin_all


def visible_mask(query_pos, key_pos, start):
    inside_query = (query_pos >= start) & (query_pos < start + PIC)
    inside_key = (key_pos >= start) & (key_pos < start + PIC)
    return (key_pos[None, :] <= query_pos[:, None]) | inside_query[:, None] & inside_key[None, :]


def norm_rows(inputs, gain_row):
    inverse = lax.rsqrt(jnp.mean(inputs * inputs, axis=-1, keepdims=True) + EPSILON)
    return (inverse, inputs * inverse * gain_row)


def norm_back(inputs, inverse, gain_row, grad_normed):
    scaled_in = inputs * inverse
    gain_grad = jnp.sum(grad_normed * scaled_in, axis=0)
    weighted = grad_normed * gain_row
    grad_in = inverse * weighted - scaled_in * inverse * jnp.mean(
        weighted * scaled_in, axis=-1, keepdims=True
    )
    return (grad_in, gain_grad)


def outer_sum(left, right):
    return jnp.einsum("ta,tb->ab", left, right, preferred_element_type=jnp.float32)


def back_dot(grad_rows, weight):
    return jnp.einsum("tb,ab->ta", grad_rows, weight, preferred_element_type=jnp.float32)


def per_device(
    layer_input,
    pic_start,
    norm_one,
    w_query,
    b_query,
    w_key,
    b_key,
    w_value,
    b_value,
    w_out,
    norm_two,
    w_gate,
    w_up,
    w_down,
    out_grad,
):
    micro_count, seq_count, row_count, model_width = layer_input.shape
    length = row_count * lax.axis_size("seq")
    tokens = seq_count * row_count
    group = HEADS // KV_HEADS
    score_scale = HD ** (-0.5)
    query_pos = lax.axis_index("seq") * row_count + jnp.arange(row_count, dtype=jnp.int32)
    key_pos = jnp.arange(length, dtype=jnp.int32)
    cosine, sine = rope_tables(jnp.tile(query_pos, seq_count), HD)

    def scores_of(query_heads, key_heads, start):
        scores = (
            jnp.einsum("rkgd,lkd->kgrl", query_heads, key_heads, preferred_element_type=jnp.float32)
            * score_scale
        )
        return jnp.where(visible_mask(query_pos, key_pos, start), scores, NEGATIVE)

    def attend_forward(element):
        q_seq, k_seq, v_seq, start = element
        query_heads = q_seq.reshape(row_count, KV_HEADS, group, HD)
        key_heads = k_seq.reshape(length, KV_HEADS, HD)
        value_heads = v_seq.reshape(length, KV_HEADS, HD)
        masked = scores_of(query_heads, key_heads, start)
        row_max = jnp.max(masked, axis=-1, keepdims=True)
        unnormed = jnp.exp(masked - row_max)
        row_total = jnp.sum(unnormed, axis=-1, keepdims=True)
        probs = (unnormed / row_total).astype(jnp.bfloat16)
        attended = jnp.einsum(
            "kgrl,lkd->rkgd", probs, value_heads, preferred_element_type=jnp.float32
        )
        return (
            attended.reshape(row_count, HEADS * HD).astype(jnp.bfloat16),
            row_max + jnp.log(row_total),
        )

    def attend_backward(element):
        q_seq, k_seq, v_seq, start, log_total, grad_seq = element
        query_heads = q_seq.reshape(row_count, KV_HEADS, group, HD)
        key_heads = k_seq.reshape(length, KV_HEADS, HD)
        value_heads = v_seq.reshape(length, KV_HEADS, HD)
        grad_heads = grad_seq.reshape(row_count, KV_HEADS, group, HD)
        probs = jnp.exp(scores_of(query_heads, key_heads, start) - log_total)
        rounded = probs.astype(jnp.bfloat16)
        prob_grad = jnp.einsum(
            "rkgd,lkd->kgrl", grad_heads, value_heads, preferred_element_type=jnp.float32
        )
        centre = jnp.sum(probs * prob_grad, axis=-1, keepdims=True)
        score_grad = (probs * (prob_grad - centre)).astype(jnp.bfloat16)
        query_grad = (
            jnp.einsum("kgrl,lkd->rkgd", score_grad, key_heads, preferred_element_type=jnp.float32)
            * score_scale
        )
        key_grad = (
            jnp.einsum(
                "kgrl,rkgd->lkd", score_grad, query_heads, preferred_element_type=jnp.float32
            )
            * score_scale
        )
        value_grad = jnp.einsum(
            "kgrl,rkgd->lkd", rounded, grad_heads, preferred_element_type=jnp.float32
        )
        return (
            query_grad.reshape(row_count, HEADS * HD),
            key_grad.reshape(length, KV_HEADS * HD),
            value_grad.reshape(length, KV_HEADS * HD),
        )

    totals = None
    outputs = []
    input_grads = []
    for micro_index in range(micro_count):
        attn_full = (
            lax.all_gather(norm_one, "dp", axis=0, tiled=True),
            lax.all_gather(w_query, "dp", axis=0, tiled=True),
            lax.all_gather(b_query, "dp", axis=0, tiled=True),
            lax.all_gather(w_key, "dp", axis=0, tiled=True),
            lax.all_gather(b_key, "dp", axis=0, tiled=True),
            lax.all_gather(w_value, "dp", axis=0, tiled=True),
            lax.all_gather(b_value, "dp", axis=0, tiled=True),
            lax.all_gather(w_out, "dp", axis=0, tiled=True),
        )
        mlp_full = (
            lax.all_gather(norm_two, "dp", axis=0, tiled=True),
            lax.all_gather(w_gate, "dp", axis=0, tiled=True),
            lax.all_gather(w_up, "dp", axis=0, tiled=True),
            lax.all_gather(w_down, "dp", axis=0, tiled=True),
        )
        gain_one, query_full, qbias_full, key_full, kbias_full, value_full, vbias_full, out_full = (
            attn_full
        )
        inputs = layer_input[micro_index].reshape(tokens, model_width).astype(jnp.float32)
        inv_one, normed_float = norm_rows(inputs, gain_one.astype(jnp.float32))
        normed = normed_float.astype(jnp.bfloat16)
        query_lin = jnp.dot(
            normed, query_full, preferred_element_type=jnp.float32
        ) + qbias_full.astype(jnp.float32)
        key_lin = jnp.dot(normed, key_full, preferred_element_type=jnp.float32) + kbias_full.astype(
            jnp.float32
        )
        value_lin = jnp.dot(
            normed, value_full, preferred_element_type=jnp.float32
        ) + vbias_full.astype(jnp.float32)
        queries = rotate(query_lin, cosine, sine, HD, 1.0).astype(jnp.bfloat16)
        keys = rotate(key_lin, cosine, sine, HD, 1.0).astype(jnp.bfloat16)
        values = value_lin.astype(jnp.bfloat16)
        keys_all, values_all = (
            lax.all_gather(
                keys.reshape(seq_count, row_count, KV_HEADS * HD), "seq", axis=1, tiled=True
            ),
            lax.all_gather(
                values.reshape(seq_count, row_count, KV_HEADS * HD), "seq", axis=1, tiled=True
            ),
        )
        query_seqs = queries.reshape(seq_count, row_count, HEADS * HD)
        starts = pic_start[micro_index]
        attended, log_total = lax.map(attend_forward, (query_seqs, keys_all, values_all, starts))
        att_rows = attended.reshape(tokens, HEADS * HD)
        resid = inputs + jnp.dot(att_rows, out_full, preferred_element_type=jnp.float32)
        gain_two, gate_full, up_full, down_full = mlp_full
        inv_two, normed_two_float = norm_rows(resid, gain_two.astype(jnp.float32))
        normed_two = normed_two_float.astype(jnp.bfloat16)
        gate_float = lax.optimization_barrier(
            jnp.dot(normed_two, gate_full, preferred_element_type=jnp.float32).astype(jnp.bfloat16)
        ).astype(jnp.float32)
        up_float = lax.optimization_barrier(
            jnp.dot(normed_two, up_full, preferred_element_type=jnp.float32).astype(jnp.bfloat16)
        ).astype(jnp.float32)
        sigmoid_gate = jax.nn.sigmoid(gate_float)
        hidden = (gate_float * sigmoid_gate * up_float).astype(jnp.bfloat16)
        output = resid + jnp.dot(hidden, down_full, preferred_element_type=jnp.float32)
        outputs.append(output.astype(jnp.bfloat16).reshape(seq_count, row_count, model_width))
        attn_back = (
            lax.all_gather(norm_one, "dp", axis=0, tiled=True),
            lax.all_gather(w_query, "dp", axis=0, tiled=True),
            lax.all_gather(b_query, "dp", axis=0, tiled=True),
            lax.all_gather(w_key, "dp", axis=0, tiled=True),
            lax.all_gather(b_key, "dp", axis=0, tiled=True),
            lax.all_gather(w_value, "dp", axis=0, tiled=True),
            lax.all_gather(b_value, "dp", axis=0, tiled=True),
            lax.all_gather(w_out, "dp", axis=0, tiled=True),
        )
        mlp_back = (
            lax.all_gather(norm_two, "dp", axis=0, tiled=True),
            lax.all_gather(w_gate, "dp", axis=0, tiled=True),
            lax.all_gather(w_up, "dp", axis=0, tiled=True),
            lax.all_gather(w_down, "dp", axis=0, tiled=True),
        )
        (
            gain_one_back,
            query_back,
            qbias_back,
            key_back,
            kbias_back,
            value_back,
            vbias_back,
            out_back,
        ) = attn_back
        gain_two_back, gate_back, up_back, down_back = mlp_back
        grad_rows = out_grad[micro_index].reshape(tokens, model_width)
        down_grad = outer_sum(hidden, grad_rows)
        hidden_grad = lax.optimization_barrier(
            back_dot(grad_rows, down_back).astype(jnp.bfloat16)
        ).astype(jnp.float32)
        gate_grad_low = (
            hidden_grad * up_float * sigmoid_gate * (1.0 + gate_float * (1.0 - sigmoid_gate))
        ).astype(jnp.bfloat16)
        up_grad_low = (hidden_grad * gate_float * sigmoid_gate).astype(jnp.bfloat16)
        gate_wgrad = outer_sum(normed_two, gate_grad_low)
        up_wgrad = outer_sum(normed_two, up_grad_low)
        grad_normed_two = back_dot(gate_grad_low, gate_back) + back_dot(up_grad_low, up_back)
        grad_middle, gain_two_grad = norm_back(
            resid, inv_two, gain_two_back.astype(jnp.float32), grad_normed_two
        )
        resid_grad = grad_rows.astype(jnp.float32) + grad_middle
        attn_grad_low = resid_grad.astype(jnp.bfloat16)
        out_wgrad = outer_sum(att_rows, attn_grad_low)
        heads_grad = back_dot(attn_grad_low, out_back).astype(jnp.bfloat16)
        query_grad, key_part, value_part = lax.map(
            attend_backward,
            (
                query_seqs,
                keys_all,
                values_all,
                starts,
                log_total,
                heads_grad.reshape(seq_count, row_count, HEADS * HD),
            ),
        )
        key_grad, value_grad = (
            lax.psum_scatter(
                key_part.astype(jnp.bfloat16), "seq", scatter_dimension=1, tiled=True
            ).astype(jnp.float32),
            lax.psum_scatter(
                value_part.astype(jnp.bfloat16), "seq", scatter_dimension=1, tiled=True
            ).astype(jnp.float32),
        )
        qlin_grad = rotate(query_grad.reshape(tokens, HEADS * HD), cosine, sine, HD, -1.0).astype(
            jnp.bfloat16
        )
        klin_grad = rotate(key_grad.reshape(tokens, KV_HEADS * HD), cosine, sine, HD, -1.0).astype(
            jnp.bfloat16
        )
        vlin_grad = value_grad.reshape(tokens, KV_HEADS * HD).astype(jnp.bfloat16)
        grad_normed = (
            back_dot(qlin_grad, query_back)
            + back_dot(klin_grad, key_back)
            + back_dot(vlin_grad, value_back)
        )
        grad_first, gain_one_grad = norm_back(
            inputs, inv_one, gain_one_back.astype(jnp.float32), grad_normed
        )
        input_grads.append((resid_grad + grad_first).reshape(seq_count, row_count, model_width))
        batch_grads = (
            gain_one_grad,
            outer_sum(normed, qlin_grad),
            jnp.sum(qlin_grad.astype(jnp.float32), axis=0),
            outer_sum(normed, klin_grad),
            jnp.sum(klin_grad.astype(jnp.float32), axis=0),
            outer_sum(normed, vlin_grad),
            jnp.sum(vlin_grad.astype(jnp.float32), axis=0),
            out_wgrad,
            gain_two_grad,
            gate_wgrad,
            up_wgrad,
            down_grad,
        )
        totals = batch_grads if totals is None else jax.tree.map(jnp.add, totals, batch_grads)
    shares = (
        lax.psum_scatter(totals[0], "dp", scatter_dimension=0, tiled=True),
        lax.psum_scatter(totals[1], "dp", scatter_dimension=0, tiled=True),
        lax.psum_scatter(totals[2], "dp", scatter_dimension=0, tiled=True),
        lax.psum_scatter(totals[3], "dp", scatter_dimension=0, tiled=True),
        lax.psum_scatter(totals[4], "dp", scatter_dimension=0, tiled=True),
        lax.psum_scatter(totals[5], "dp", scatter_dimension=0, tiled=True),
        lax.psum_scatter(totals[6], "dp", scatter_dimension=0, tiled=True),
        lax.psum_scatter(totals[7], "dp", scatter_dimension=0, tiled=True),
        lax.psum_scatter(totals[8], "dp", scatter_dimension=0, tiled=True),
        lax.psum_scatter(totals[9], "dp", scatter_dimension=0, tiled=True),
        lax.psum_scatter(totals[10], "dp", scatter_dimension=0, tiled=True),
        lax.psum_scatter(totals[11], "dp", scatter_dimension=0, tiled=True),
    )
    shares = (
        lax.psum(shares[0].astype(jnp.bfloat16), "seq").astype(jnp.float32),
        lax.psum(shares[1].astype(jnp.bfloat16), "seq").astype(jnp.float32),
        lax.psum(shares[2].astype(jnp.bfloat16), "seq").astype(jnp.float32),
        lax.psum(shares[3].astype(jnp.bfloat16), "seq").astype(jnp.float32),
        lax.psum(shares[4].astype(jnp.bfloat16), "seq").astype(jnp.float32),
        lax.psum(shares[5].astype(jnp.bfloat16), "seq").astype(jnp.float32),
        lax.psum(shares[6].astype(jnp.bfloat16), "seq").astype(jnp.float32),
        lax.psum(shares[7].astype(jnp.bfloat16), "seq").astype(jnp.float32),
        lax.psum(shares[8].astype(jnp.bfloat16), "seq").astype(jnp.float32),
        lax.psum(shares[9].astype(jnp.bfloat16), "seq").astype(jnp.float32),
        lax.psum(shares[10].astype(jnp.bfloat16), "seq").astype(jnp.float32),
        lax.psum(shares[11].astype(jnp.bfloat16), "seq").astype(jnp.float32),
    )
    return (
        jnp.stack(outputs),
        jnp.stack(input_grads),
        shares[0],
        shares[1],
        shares[2],
        shares[3],
        shares[4],
        shares[5],
        shares[6],
        shares[7],
        shares[8],
        shares[9],
        shares[10],
        shares[11],
    )


def solution(mesh):
    placed = (
        P(None, "dp", "seq", None),
        P(None, "dp"),
        P("dp"),
        P("dp", None),
        P("dp"),
        P("dp", None),
        P("dp"),
        P("dp", None),
        P("dp"),
        P("dp", None),
        P("dp"),
        P("dp", None),
        P("dp", None),
        P("dp", None),
        P(None, "dp", "seq", None),
    )
    return jax.shard_map(
        per_device,
        mesh=mesh,
        in_specs=placed,
        out_specs=(
            P(None, "dp", "seq", None),
            P(None, "dp", "seq", None),
            P("dp"),
            P("dp", None),
            P("dp"),
            P("dp", None),
            P("dp"),
            P("dp", None),
            P("dp"),
            P("dp", None),
            P("dp"),
            P("dp", None),
            P("dp", None),
            P("dp", None),
        ),
        check_vma=False,
    )
```

profile of v0, /device:TPU:9, one launch (start us, length us, event | category | flops | bytes accessed | tf_op | source)
XLA Modules:
  0.0 1241.6 jit_solution(1288814986106040895)
XLA Ops:
  20.1 35.4 %all-reduce.18 = (bf16[128]{0:T(256)(128)(2,1)S(1)}, bf16[896]{0:T(1024)(128)(2,1)S(1)}, bf16[128]{0:T(256)(128)(2,1)S(1)}, bf16[896]{0:T(1024)(128)(2,1)S(1)}, bf16[896]{0:T(1024)(128)(2,1)S(1)}) all-reduce(bf16[128]{0:T(256)(128)(2,1)S(1)} %dynamic-update-slice.1, ...), channel_id=1, replica_groups=mesh['dp'=16,'seq'=8] {'dp'}, use_global_device_ids=true, to_apply=%add.1 | all-reduce | flops 2944 | bytes 11776
  55.5 17.4 %all_gather.33 = bf16[896,128]{1,0:T(8,128)(2,1)S(1)} all-gather(bf16[56,128]{1,0:T(8,128)(2,1)} %param.22), channel_id=1, replica_groups=mesh['dp'=16,'seq'=8] {'dp'}, dimensions={0}, use_global_device_ids=true | all-gather | bytes 243712 | tf_op jit(solution)/shard_map/all_gather | solution.py:161
  73.4 24.6 %all-gather = bf16[1024,128]{1,0:T(8,128)(2,1)S(1)} all-gather(bf16[128,128]{1,0:T(8,128)(2,1)S(1)} %fusion.60), channel_id=2, replica_groups=mesh['dp'=16,'seq'=8] {'seq'}, dimensions={0}, use_global_device_ids=true | all-gather | bytes 294912 | tf_op jit(solution)/shard_map/all_gather | solution.py:193
  99.2 12.8 %all-gather.2 = bf16[1024,128]{1,0:T(8,128)(2,1)S(1)} all-gather(bf16[128,128]{1,0:T(8,128)(2,1)S(1)} %fusion.61), channel_id=4, replica_groups=mesh['dp'=16,'seq'=8] {'seq'}, dimensions={0}, use_global_device_ids=true | all-gather | bytes 294912 | tf_op jit(solution)/shard_map/all_gather | solution.py:193
  115.1 19.1 %all_gather.36 = bf16[896,128]{1,0:T(8,128)(2,1)S(1)} all-gather(bf16[56,128]{1,0:T(8,128)(2,1)S(1)} %copy-done.68), channel_id=1, replica_groups=mesh['dp'=16,'seq'=8] {'dp'}, dimensions={0}, use_global_device_ids=true | all-gather | bytes 243712 | tf_op jit(solution)/shard_map/all_gather | solution.py:159
  137.5 16.0 %all-gather.1 = bf16[1024,128]{0,1:T(8,128)(2,1)S(1)} all-gather(bf16[128,128]{0,1:T(8,128)(2,1)S(1)} %get-tuple-element.208), channel_id=3, replica_groups=mesh['dp'=16,'seq'=8] {'seq'}, dimensions={0}, use_global_device_ids=true | all-gather | bytes 294912 | tf_op jit(solution)/shard_map/all_gather | solution.py:190
  153.5 12.5 %all-gather.3 = bf16[1024,128]{0,1:T(8,128)(2,1)} all-gather(bf16[128,128]{0,1:T(8,128)(2,1)S(1)} %get-tuple-element.209), channel_id=5, replica_groups=mesh['dp'=16,'seq'=8] {'seq'}, dimensions={0}, use_global_device_ids=true | all-gather | bytes 294912 | tf_op jit(solution)/shard_map/all_gather | solution.py:190
  194.0 7.5 convolution_convert_fusion
  204.0 46.5 %all-gather.16.cloned.1.call-done = bf16[896,4864]{1,0:T(8,128)(2,1)} async-done(((bf16[56,4864]{1,0:T(8,128)(2,1)}), bf16[896,4864]{1,0:T(8,128)(2,1)}) %all-gather.16.cloned.1.call-update) | async-done | bytes 8716304 | tf_op jit(solution)/shard_map/all_gather | solution.py:168
  250.4 4.9 convolution_convert_fusion.4
  255.4 69.0 %all-gather.14.cloned.1.call-done = bf16[896,4864]{1,0:T(8,128)(2,1)} async-done(((bf16[56,4864]{1,0:T(8,128)(2,1)}), bf16[896,4864]{1,0:T(8,128)(2,1)}) %all-gather.14.cloned.1.call-update) | async-done | bytes 8716304 | tf_op jit(solution)/shard_map/all_gather | solution.py:167
  324.4 5.1 convolution_convert_fusion.5
  329.6 7.4 fusion.168
  337.1 4.7 multiply_reduce_fusion.1
  356.7 7.5 fusion
  375.8 7.7 fusion.3
  383.6 4.7 fusion.5
  422.4 10.4 fusion.166
  432.8 14.6 %convolution_add_fusion.2 = f32[896,4864]{1,0:T(8,128)} fusion(f32[896,4864]{1,0:T(8,128)} %fusion.166, bf16[128,896]{1,0:T(8,128)(2,1)S(1)} %copy-done.26, bf16[128,4864]{1,0:T(8,128)(2,1)S(1)} %copy-done.18, bf16[128,4864]{1,0:T(8,128)(2,1)S(1)} %copy-done.24, bf16[128,4864]{1,0:T(8,128)(2,1)S(1)} %convolution_convert_fusion.3), kind=kOutput, calls=%fused_computation.2 | convolution fusion | flops 1128136704 | bytes 38830080 | tf_op jit(solution)/shard_map/ta,tb->ab/dot_general | solution.py:61
  451.6 10.3 convolution_add_fusion.1
  466.5 10.4 convolution_add_fusion
  480.4 5.3 fusion.59
  503.0 77.1 %reduce-scatter.48.cloned.1.call-done = f32[56,896]{1,0:T(8,128)} async-done(((f32[896,896]{1,0:T(8,128)}), f32[56,896]{1,0:T(8,128)}) %reduce-scatter.48.cloned.1.call-update) | async-done | bytes 200720
  581.6 79.3 %reduce-scatter.42.cloned.1.call-done = f32[56,896]{1,0:T(8,128)} async-done(((f32[896,896]{1,0:T(8,128)}), f32[56,896]{1,0:T(8,128)}) %reduce-scatter.42.cloned.1.call-update) | async-done | bytes 200720
  662.5 116.6 %reduce-scatter.50.cloned.1.call-done = f32[56,4864]{1,0:T(8,128)} async-done(((f32[896,4864]{1,0:T(8,128)}), f32[56,4864]{1,0:T(8,128)}) %reduce-scatter.50.cloned.1.call-update) | async-done | bytes 1089552
  781.2 115.6 %reduce-scatter.52.cloned.1.call-done = f32[56,4864]{1,0:T(8,128)} async-done(((f32[896,4864]{1,0:T(8,128)}), f32[56,4864]{1,0:T(8,128)}) %reduce-scatter.52.cloned.1.call-update) | async-done | bytes 1089552
  899.0 115.2 %reduce-scatter.54.cloned.1.call-done = f32[304,896]{1,0:T(8,128)} async-done(((f32[4864,896]{1,0:T(8,128)}), f32[304,896]{1,0:T(8,128)}) %reduce-scatter.54.cloned.1.call-update) | async-done | bytes 1089552
  1016.4 58.5 %all-reduce.17 = (bf16[896]{0:T(1024)(128)(2,1)S(1)}, bf16[896]{0:T(1024)(128)(2,1)S(1)}, bf16[128]{0:T(256)(128)(2,1)S(1)}, bf16[128]{0:T(256)(128)(2,1)S(1)}, bf16[896]{0:T(1024)(128)(2,1)S(1)}) all-reduce(f32[896]{0:T(1024)S(1)} %add.367, f32[896]{0:T(1024)S(1)} %add.372, ...), channel_id=10, replica_groups=mesh['dp'=16,'seq'=8] {'dp'}, use_global_device_ids=true, to_apply=%region_20.21.clone | all-reduce | flops 2944 | bytes 17664
  1076.6 10.3 reduce-scatter.46.cloned.1.call-done
  1087.7 72.9 %reduce-scatter.44.cloned.1.call-done = f32[56,128]{1,0:T(8,128)} async-done(((f32[896,128]{1,0:T(8,128)}), f32[56,128]{1,0:T(8,128)}) %reduce-scatter.44.cloned.1.call-update) | async-done | bytes 28688
  1161.4 21.7 %all-reduce.19 = (bf16[56]{0:T(256)(128)(2,1)S(1)}, bf16[56]{0:T(256)(128)(2,1)S(1)}, bf16[56,128]{1,0:T(8,128)(2,1)S(1)}, bf16[8]{0:T(256)(128)(2,1)S(1)}, bf16...) all-reduce(bf16[56]{0:T(256)(128)(2,1)S(1)} %dynamic-slice.44, ...), channel_id=1, replica_groups=mesh['dp'=16,'seq'=8] {'seq'}, use_global_device_ids=true, to_apply=%region_21.22 | all-reduce | flops 14520 | bytes 58080 | tf_op jit(solution)/shard_map/psum | solution.py:326
  1186.8 40.2 %all-reduce.23.cloned.1.call-done = (bf16[56,896]{1,0:T(8,128)(2,1)}, bf16[56,896]{1,0:T(8,128)(2,1)}, bf16[56,4864]{1,0:T(8,128)(2,1)}, bf16[56,4864]{1,0:T(8,128)(2,1)}, bf16[304,896]{1,0:T(8,128)(2,1)}) async-done(((bf16[56,896]{1,0:T(8,128)(2,1)}, bf16[56,896]{1,0:T(8,128)(2,1)}, bf16[56,4864]{1,0:T(8,128)(2,1)}, bf16[56,4864]{1,0:T(8,128)(2,1)}, bf16[304,896]{1,0:T(8,128)(2,1)}), ...) | async-done | bytes 1835024 | tf_op jit(solution)/shard_map/psum | solution.py:327
  (384 shorter events, 160.2 us)
Async XLA Ops:
  7.2 65.8 %copy-start.12 = (bf16[2,1,128,896]{3,2,1,0:T(8,128)(2,1)S(1)}, bf16[2,1,128,896]{3,2,1,0:T(8,128)(2,1)}, u32[]{:S(2)}) copy-start(bf16[2,1,128,896]{3,2,1,0:T(8,128)(2,1)} %param.15) | copy-start | bytes 1376260
  7.2 159.8 %all-gather.10.cloned.1.call-start = ((), (), s32[]{:S(2)}) async-start(), calls=%async_computation.11 | async-start | bytes 1705984 | tf_op jit(solution)/shard_map/all_gather | solution.py:157
  7.9 176.7 %all-gather.12.cloned.1.call-start = ((), (), s32[]{:S(2)}) async-start(), calls=%async_computation.12 | async-start | bytes 1705984 | tf_op jit(solution)/shard_map/all_gather | solution.py:163
  8.7 185.0 %all-gather.18.cloned.1.call-start = ((), (), s32[]{:S(2)}) async-start(), calls=%async_computation.15 | async-start | bytes 9261056 | tf_op jit(solution)/shard_map/all_gather | solution.py:169
  9.4 241.0 %all-gather.16.cloned.1.call-start = ((), (), s32[]{:S(2)}) async-start(), calls=%async_computation.14 | async-start | bytes 9261056 | tf_op jit(solution)/shard_map/all_gather | solution.py:168
  10.0 314.4 %all-gather.14.cloned.1.call-start = ((), (), s32[]{:S(2)}) async-start(), calls=%async_computation.13 | async-start | bytes 9261056 | tf_op jit(solution)/shard_map/all_gather | solution.py:167
  10.6 479.4 %reduce-scatter.38.cloned.1.call-start = ((), (), s32[]{:S(2)}) async-start(), calls=%async_computation.18 | async-start | bytes 294912
  73.0 39.9 %copy-start.63 = (bf16[896,128]{1,0:T(8,128)(2,1)}, bf16[896,128]{1,0:T(8,128)(2,1)S(1)}, u32[]{:S(2)}) copy-start(bf16[896,128]{1,0:T(8,128)(2,1)S(1)} %all_gather.33) | copy-start | bytes 688132
  98.0 17.1 %copy-start.68 = (bf16[56,128]{1,0:T(8,128)(2,1)S(1)}, bf16[56,128]{1,0:T(8,128)(2,1)}, u32[]{:S(2)}) copy-start(bf16[56,128]{1,0:T(8,128)(2,1)} %param.20) | copy-start | bytes 43012
  113.1 21.9 %copy-start.54 = (f32[128,64]{0,1:T(8,128)}, f32[128,64]{0,1:T(8,128)S(1)}, u32[]{:S(2)}) copy-start(f32[128,64]{0,1:T(8,128)S(1)} %get-tuple-element.216) | copy-start | bytes 98308
  113.1 21.8 %copy-start.56 = (f32[128,64]{0,1:T(8,128)}, f32[128,64]{0,1:T(8,128)S(1)}, u32[]{:S(2)}) copy-start(f32[128,64]{0,1:T(8,128)S(1)} %get-tuple-element.217) | copy-start | bytes 98308
  153.5 33.9 %copy-start.40 = (bf16[1024,128]{0,1:T(8,128)(2,1)}, bf16[1024,128]{0,1:T(8,128)(2,1)S(1)}, u32[]{:S(2)}) copy-start(bf16[1024,128]{0,1:T(8,128)(2,1)S(1)} %all-gather.1) | copy-start | bytes 786436
  204.0 133.0 %copy-start.22 = (bf16[128,4864]{1,0:T(8,128)(2,1)}, bf16[128,4864]{1,0:T(8,128)(2,1)S(1)}, u32[]{:S(2)}) copy-start(bf16[128,4864]{1,0:T(8,128)(2,1)S(1)} %convolution_convert_fusion.1) | copy-start | bytes 3735556
  255.4 74.1 %copy-start.20 = (bf16[128,4864]{1,0:T(8,128)(2,1)}, bf16[128,4864]{1,0:T(8,128)(2,1)S(1)}, u32[]{:S(2)}) copy-start(bf16[128,4864]{1,0:T(8,128)(2,1)S(1)} %convolution_convert_fusion.4) | copy-start | bytes 3735556
  324.4 12.6 %slice-start.4 = ((s8[8716288]{0:T(1024)(128)(4,1)}), s8[4194304]{0:T(1024)(128)(4,1)S(1)}, s32[]{:S(2)}) async-start(s8[8716288]{0:T(1024)(128)(4,1)} %bitcast.431), calls=%async_computation.32 | async-start | bytes 8388608
  324.4 12.6 %slice-start.5 = ((s8[8716288]{0:T(1024)(128)(4,1)}), s8[4194304]{0:T(1024)(128)(4,1)S(1)}, s32[]{:S(2)}) async-start(s8[8716288]{0:T(1024)(128)(4,1)} %bitcast.431), calls=%async_computation.33 | async-start | bytes 8388608
  345.1 87.7 %copy-start.6 = (bf16[128,4864]{1,0:T(8,128)(2,1)}, bf16[128,4864]{1,0:T(8,128)(2,1)S(1)}, u32[]{:S(2)}) copy-start(bf16[128,4864]{1,0:T(8,128)(2,1)S(1)} %convolution_convert_fusion.3) | copy-start | bytes 3735556
  353.7 10.5 copy-start.44
  375.6 115.4 %reduce-scatter.34.cloned.1.call-start = ((), (), s32[]{:S(2)}) async-start(), calls=%async_computation.16 | async-start | bytes 294912
  395.0 97.0 %reduce-scatter.36.cloned.1.call-start = ((), (), s32[]{:S(2)}) async-start(), calls=%async_computation.17 | async-start | bytes 294912
  400.8 96.3 %reduce-scatter.40.cloned.1.call-start = ((), (), s32[]{:S(2)}) async-start(), calls=%async_computation.19 | async-start | bytes 294912
  406.4 173.6 %reduce-scatter.48.cloned.1.call-start = ((), (), s32[]{:S(2)}) async-start(), calls=%async_computation.23 | async-start | bytes 3411968
  411.3 249.6 %reduce-scatter.42.cloned.1.call-start = ((), (), s32[]{:S(2)}) async-start(), calls=%async_computation.20 | async-start | bytes 3411968
  421.2 11.7 copy-start.26
  421.2 358.0 %reduce-scatter.50.cloned.1.call-start = ((), (), s32[]{:S(2)}) async-start(), calls=%async_computation.24 | async-start | bytes 18522112
  447.4 449.4 %reduce-scatter.52.cloned.1.call-start = ((), (), s32[]{:S(2)}) async-start(), calls=%async_computation.25 | async-start | bytes 18522112
  462.0 552.2 %reduce-scatter.54.cloned.1.call-start = ((), (), s32[]{:S(2)}) async-start(), calls=%async_computation.26 | async-start | bytes 18522112
  477.0 609.9 %reduce-scatter.46.cloned.1.call-start = ((), (), s32[]{:S(2)}) async-start(), calls=%async_computation.22 | async-start | bytes 487424
  499.6 661.0 %reduce-scatter.44.cloned.1.call-start = ((), (), s32[]{:S(2)}) async-start(), calls=%async_computation.21 | async-start | bytes 487424
  501.3 725.8 %all-reduce.23.cloned.1.call-start = ((), (), s32[]{:S(2)}) async-start(), calls=%async_computation.27 | async-start | bytes 3670016 | tf_op jit(solution)/shard_map/psum | solution.py:327
  781.2 294.1 %copy-start.29 = (f32[128,896]{1,0:T(8,128)S(1)}, f32[128,896]{1,0:T(8,128)}, u32[]{:S(2)}) copy-start(f32[128,896]{1,0:T(8,128)} %copy-done.27) | copy-start | bytes 1376260
  781.2 294.1 %copy-start.32 = (f32[128,896]{1,0:T(8,128)S(1)}, f32[128,896]{1,0:T(8,128)}, u32[]{:S(2)}) copy-start(f32[128,896]{1,0:T(8,128)} %copy-done.30) | copy-start | bytes 1376260
  (68 other events, 305.7 us)
Sparse Core Ops, SparseCore 0:
  10.2 45.4 all-gather.9
  57.8 43.5 all-gather.11
  103.6 72.7 all-gather.17
  178.4 71.9 all-gather.15
  252.4 71.9 all-gather.13
  375.7 25.8 reduce-scatter.37
  404.1 29.3 reduce-scatter.33
  435.8 29.3 reduce-scatter.35
  467.7 29.3 reduce-scatter.39
  500.4 79.5 reduce-scatter.47
  583.5 77.3 reduce-scatter.41
  664.3 114.8 reduce-scatter.49
  783.0 113.8 reduce-scatter.51
  900.2 113.9 reduce-scatter.53
  1017.5 69.3 reduce-scatter.45
  1090.0 70.5 reduce-scatter.43
  1164.5 62.4 all-reduce.22
where the time goes:
time: 1250 us; the launch traced here: 1240 us
  waiting for transfers between devices  750 us (60%)
  blocking collectives  218 us (17%)
  matrix products  164 us (13%)
  other arithmetic  48.1 us (4%)
  local copies, waits for them, and re-layouts  39.5 us (3%)
  between operations  20.2 us (2%)
    unnamed x28, waiting for transfers between devices  595 us
    unnamed x2, blocking collectives  93.9 us
    all_gather x1, waiting for transfers between devices, per_device(): lax.all_gather(w_gate, 'dp', axis=0, tiled=True)  69 us
    dot_general x14, matrix products, outer_sum(): jnp.einsum('ta,tb->ab', left, right, preferred_element_type=jnp.float32)  64.8 us
    all_gather x1, waiting for transfers between devices, per_device(): lax.all_gather(w_up, 'dp', axis=0, tiled=True)  46.5 us
    psum x1, waiting for transfers between devices, per_device(): lax.psum(shares[1].astype(jnp.bfloat16), 'seq').astype(jnp.float32)  40.2 us
    all_gather x2, blocking collectives, per_device(): lax.all_gather(values.reshape(seq_count, row_count, KV_HEADS * HD), 'seq'...  37.4 us
    dot_general x14, matrix products, back_dot(): jnp.einsum('tb,ab->ta', grad_rows, weight, preferred_element_type=jnp.flo...  33.3 us
  transfers between devices with their start and end apart: 17, of which 11 were waited for; matrix products, arithmetic and copies ran while one was open for 15% of the time, Pallas kernels for 0%

commit v1 on v0

v1 whole, which is shorter than its diff:
```python
import functools

import jax
import jax.numpy as jnp
import numpy as np
from jax import lax
from jax.experimental import pallas as pl
from jax.experimental.pallas import tpu as pltpu
from jax.sharding import PartitionSpec as P

HEADS = 14
KV_HEADS = 2
HD = 64
PIC = 256
D = 896
FF = 4864
ROWS = 256
LANE = 128
SHARD = 56
FFS = 1280
DROWS = 304
DHALF = 152
QKV = 1152
PACK = 2304
EPSILON = 1e-06
ROPE_BASE = 1000000.0
NEGATIVE = -1e30
MESH = pl.DeviceIdType.MESH
BF = jnp.bfloat16
F32 = jnp.float32
VLIM = 60 * 1024 * 1024
UNIT0 = (0, 9, 19, 28)


def place():
    dp = lax.axis_index("dp")
    seq = lax.axis_index("seq")
    return dp // 4, dp % 4, seq // 2, seq % 2


def at(z, x, y, c):
    return ((z % 4) * 4 + x % 4, (y % 4) * 2 + c % 2)


def peers_of(axis):
    z, x, y, c = place()
    moves = (1, 3, 2)
    if axis == "z":
        return [at(z + m, x, y, c) for m in moves]
    if axis == "x":
        return [at(z, x + m, y, c) for m in moves]
    if axis == "y":
        return [at(z, x, y + m, c) for m in moves]
    return [at(z, x, y, c + 1)]


def greet(axes):
    barrier = pltpu.get_barrier_semaphore()
    count = 0
    for axis in axes:
        for peer in peers_of(axis):
            pl.semaphore_signal(barrier, inc=1, device_id=peer, device_id_type=MESH)
            count += 1
    pl.semaphore_wait(barrier, count)


def remote(src, dst, send, recv, peer):
    return pltpu.make_async_remote_copy(
        src_ref=src, dst_ref=dst, send_sem=send, recv_sem=recv, device_id=peer, device_id_type=MESH
    )


def start(copies):
    for copy in copies:
        copy.start()


def wait_recv(copies):
    for copy in copies:
        copy.wait_recv()


def wait_send(copies):
    for copy in copies:
        copy.wait_send()


def ring_copies(src, dst, ss, rs, axis):
    return [remote(src, dst, ss.at[k], rs.at[k], peer) for k, peer in enumerate(peers_of(axis))]


def outer_sum(left, right):
    return jnp.einsum("ta,tb->ab", left, right, preferred_element_type=F32)


def back_dot(grad_rows, weight):
    return jnp.einsum("tb,ab->ta", grad_rows, weight, preferred_element_type=F32)


def gather_kernel(
    p_ref, wg_ref, wu_ref, wd_ref, g_ref,
    p4, w4, wd, ga,
    zero, loc, ss, rs, dss, drs,
):
    z, x, y, c = place()
    greet(("z", "x", "y", "c"))
    zero[...] = jnp.zeros_like(zero)
    first = pl.multiple_of(((19 * y) // 2) * LANE, LANE)
    off = 64 * (y % 2)

    def down_rows(xx, cc):
        return pl.ds(pl.multiple_of(off + DROWS * xx + DHALF * cc, 8), DHALF)

    base = c * QKV
    mine = pl.ds(pl.multiple_of(base, LANE), QKV)
    locals_ = [
        pltpu.make_async_copy(p_ref.at[:, mine], p4.at[z, x, :, mine], loc.at[0]),
        pltpu.make_async_copy(g_ref, ga.at[y], loc.at[1]),
        pltpu.make_async_copy(
            zero, wd.at[pl.ds(pl.multiple_of(1216 * (1 - y % 2), 8), 64)], loc.at[2]
        ),
    ]
    start(locals_)
    own_w = [
        pltpu.make_async_copy(ref.at[:, pl.ds(first, FFS)], w4.at[c, z, x], loc.at[3])
        for ref in (wg_ref, wu_ref)
    ]

    @pl.when(c == 0)
    def _():
        own_w[0].start()

    @pl.when(c == 1)
    def _():
        own_w[1].start()

    cols_a = pl.ds(pl.multiple_of(base, LANE), 640)
    cols_b = pl.ds(pl.multiple_of(base + 640, LANE), 512)
    pa1 = ring_copies(p_ref.at[:, cols_a], p4.at[z, x, :, cols_a], ss.at[0], rs.at[0], "x")
    pb1 = ring_copies(p_ref.at[:, cols_b], p4.at[z, x, :, cols_b], ss.at[1], rs.at[1], "z")
    start(pa1)
    start(pb1)
    half = [pl.ds(0, 640), pl.ds(640, 640)]
    wa1 = ring_copies(w4.at[c, z, x, :, half[0]], w4.at[c, z, x, :, half[0]], ss.at[2], rs.at[2], "x")
    wb1 = ring_copies(w4.at[c, z, x, :, half[1]], w4.at[c, z, x, :, half[1]], ss.at[3], rs.at[3], "z")
    for copy in locals_ + own_w[:1]:
        copy.wait()
    start(wa1)
    start(wb1)
    own = down_rows(x, c)
    own_src = pl.ds(pl.multiple_of(DHALF * c, 8), DHALF)
    dz = [
        remote(wd_ref.at[own_src], wd.at[own], dss.at[k], drs.at[0], peer)
        for k, peer in enumerate(peers_of("z"))
    ]
    dloc = pltpu.make_async_copy(wd_ref.at[own_src], wd.at[own], loc.at[5])

    @pl.when(z == y)
    def _():
        dloc.start()
        start(dz)

    gy = ring_copies(g_ref, ga.at[y], ss.at[8], rs.at[8], "y")
    start(gy)

    pa2 = ring_copies(p4.at[z, :, :, cols_a], p4.at[z, :, :, cols_a], ss.at[4], rs.at[4], "z")
    pb2 = ring_copies(p4.at[:, x, :, cols_b], p4.at[:, x, :, cols_b], ss.at[5], rs.at[5], "x")
    wa2 = ring_copies(w4.at[c, z, :, :, half[0]], w4.at[c, z, :, :, half[0]], ss.at[6], rs.at[6], "z")
    wb2 = ring_copies(w4.at[c, :, x, :, half[1]], w4.at[c, :, x, :, half[1]], ss.at[7], rs.at[7], "x")
    wait_recv(pa1)
    start(pa2)
    wait_recv(pb1)
    start(pb2)
    wait_recv(wa1)
    start(wa2)
    wait_recv(wb1)
    start(wb2)

    @pl.when(z == y)
    def _():
        dloc.wait()

    @pl.when(z != y)
    def _():
        dz[0].wait_recv()

    dx = ring_copies(wd.at[own], wd.at[own], dss.at[pl.ds(3, 3)], drs.at[pl.ds(1, 3)], "x")
    start(dx)
    sibling = peers_of("c")[0]
    wait_recv(pa2)
    wait_recv(pb2)
    psib = remote(p4.at[:, :, :, mine], p4.at[:, :, :, mine], dss.at[6], drs.at[4], sibling)
    psib.start()
    wait_recv(wa2)
    wait_recv(wb2)
    wsib = remote(w4.at[c], w4.at[c], dss.at[7], drs.at[5], sibling)
    wsib.start()
    wait_recv(dx)
    dsib = [
        remote(wd.at[down_rows(xx, c)], wd.at[down_rows(xx, c)], dss.at[8 + xx], drs.at[6 + xx], sibling)
        for xx in range(4)
    ]
    start(dsib)
    wait_recv(gy)
    psib.wait_recv()
    wsib.wait_recv()
    wait_recv(dsib)

    @pl.when(z == y)
    def _():
        wait_send(dz)

    for group in (pa1, pb1, wa1, wb1, pa2, pb2, wa2, wb2, gy, dx, [psib], [wsib], dsib):
        wait_send(group)


def gather_all(pack, w_gate, w_up, w_down, grads):
    anyspec = pl.BlockSpec(memory_space=pl.ANY)
    return pl.pallas_call(
        gather_kernel,
        out_shape=(
            jax.ShapeDtypeStruct((4, 4, SHARD, PACK), BF),
            jax.ShapeDtypeStruct((2, 4, 4, SHARD, FFS), BF),
            jax.ShapeDtypeStruct((FFS, D), BF),
            jax.ShapeDtypeStruct((4, ROWS, D), BF),
        ),
        in_specs=[anyspec] * 5,
        out_specs=(anyspec,) * 4,
        scratch_shapes=[
            pltpu.VMEM((64, D), BF),
            pltpu.SemaphoreType.DMA((6,)),
            pltpu.SemaphoreType.DMA((9, 3)),
            pltpu.SemaphoreType.DMA((9, 3)),
            pltpu.SemaphoreType.DMA((12,)),
            pltpu.SemaphoreType.DMA((10,)),
        ],
        compiler_params=pltpu.CompilerParams(
            collective_id=0, has_side_effects=True, vmem_limit_bytes=VLIM
        ),
        name="gather_weights",
    )(pack, w_gate, w_up, w_down, grads)


def mlp_kernel(
    x_ref, ga_ref, w_ref, wd_ref, resid_ref,
    out_ref, ng_ref, dw_ref, dwd_ref,
    xall, hid, gg, ug, outp, ngp, outr, ngr, xt, acc_out, ss, rs,
):
    z, x, y, c = place()
    greet(("y",))
    xall[y] = x_ref[...]
    xs = ring_copies(xall.at[y], xall.at[y], ss.at[0], rs.at[0], "y")
    start(xs)

    def hop(k):
        return jnp.where(k == 1, 3, jnp.where(k == 2, 1, jnp.where(k == 3, 2, 0)))

    def send_back(buf, dst, k, group):
        yk = y + hop(k)
        return remote(
            buf.at[k], dst.at[jnp.maximum(k - 1, 0)], ss.at[group, jnp.maximum(k - 1, 0)],
            rs.at[group, jnp.maximum(k - 1, 0)], at(z, x, yk, c),
        )

    def block(k, carry):
        yk = (y + hop(k)) % 4

        @pl.when(k > 0)
        def _():
            index = jnp.maximum(k - 1, 0)
            remote(
                xall.at[y], xall.at[y], ss.at[0, index], rs.at[0, index], at(z, x, y + 1, c)
            ).wait_recv()

        rows = pl.ds(pl.multiple_of(k * ROWS, ROWS), ROWS)

        def tile(n, carry):
            cols = pl.ds(pl.multiple_of(n * 256, 256), 256)
            xb = xall[yk]
            gb = ga_ref[yk]
            gate = jnp.dot(xb, w_ref[0, :, cols], preferred_element_type=F32).astype(BF).astype(F32)
            up = jnp.dot(xb, w_ref[1, :, cols], preferred_element_type=F32).astype(BF).astype(F32)
            hg = lax.dot_general(
                gb, wd_ref[cols, :], (((1,), (1,)), ((), ())), preferred_element_type=F32
            ).astype(BF).astype(F32)
            sig = jax.nn.sigmoid(gate)
            act = gate * sig
            hid[rows, cols] = (act * up).astype(BF)
            ug[rows, cols] = (hg * act).astype(BF)
            gg[rows, cols] = (hg * up * sig * (1.0 + gate * (1.0 - sig))).astype(BF)
            return carry

        lax.fori_loop(0, 5, tile, 0)
        ngp_f = lax.dot_general(
            gg[rows, :], w_ref[0], (((1,), (1,)), ((), ())), preferred_element_type=F32
        ) + lax.dot_general(
            ug[rows, :], w_ref[1], (((1,), (1,)), ((), ())), preferred_element_type=F32
        )

        @pl.when(k == 0)
        def _():
            ng_ref[...] = ngp_f

        @pl.when(k > 0)
        def _():
            ngp[k] = ngp_f.astype(BF)
            send_back(ngp, ngr, k, 1).start()

        out_f = jnp.dot(hid[rows, :], wd_ref[...], preferred_element_type=F32)

        @pl.when(k == 0)
        def _():
            acc_out[...] = resid_ref[...] + out_f

        @pl.when(k > 0)
        def _():
            outp[k] = out_f.astype(BF)
            send_back(outp, outr, k, 2).start()

        xt[:, rows] = xall[yk].T
        return carry

    lax.fori_loop(0, 4, block, 0)

    def wtile(n, carry):
        cols = pl.ds(pl.multiple_of(n * 256, 256), 256)
        dw_ref[0, :, cols] = jnp.dot(xt[...], gg[:, cols], preferred_element_type=F32).astype(BF)
        dw_ref[1, :, cols] = jnp.dot(xt[...], ug[:, cols], preferred_element_type=F32).astype(BF)
        acc = jnp.zeros((256, D), F32)
        for k in range(4):
            yk = (y + (0, 3, 1, 2)[k]) % 4
            acc += lax.dot_general(
                hid[pl.ds(k * ROWS, ROWS), cols], ga_ref[yk], (((0,), (0,)), ((), ())),
                preferred_element_type=F32,
            )
        dwd_ref[cols, :] = acc.astype(BF)
        return carry

    lax.fori_loop(0, 5, wtile, 0)
    for k in (1, 2, 3):
        send_back(ngp, ngr, k, 1).wait_recv()
    ng_ref[...] = (
        ng_ref[...] + ngr[0].astype(F32) + ngr[1].astype(F32) + ngr[2].astype(F32)
    )
    for k in (1, 2, 3):
        send_back(outp, outr, k, 2).wait_recv()
    out_ref[...] = (
        acc_out[...] + outr[0].astype(F32) + outr[1].astype(F32) + outr[2].astype(F32)
    ).astype(BF)
    wait_send(xs)
    for k in (1, 2, 3):
        send_back(ngp, ngr, k, 1).wait_send()
        send_back(outp, outr, k, 2).wait_send()


def feed_forward(normed_two, ga, w2, wd, resid):
    vm = pl.BlockSpec(memory_space=pltpu.VMEM)
    return pl.pallas_call(
        mlp_kernel,
        out_shape=(
            jax.ShapeDtypeStruct((ROWS, D), BF),
            jax.ShapeDtypeStruct((ROWS, D), F32),
            jax.ShapeDtypeStruct((2, D, FFS), BF),
            jax.ShapeDtypeStruct((FFS, D), BF),
        ),
        in_specs=[vm] * 5,
        out_specs=(vm,) * 4,
        scratch_shapes=[
            pltpu.VMEM((4, ROWS, D), BF),
            pltpu.VMEM((4 * ROWS, FFS), BF),
            pltpu.VMEM((4 * ROWS, FFS), BF),
            pltpu.VMEM((4 * ROWS, FFS), BF),
            pltpu.VMEM((4, ROWS, D), BF),
            pltpu.VMEM((4, ROWS, D), BF),
            pltpu.VMEM((3, ROWS, D), BF),
            pltpu.VMEM((3, ROWS, D), BF),
            pltpu.VMEM((D, 4 * ROWS), BF),
            pltpu.VMEM((ROWS, D), F32),
            pltpu.SemaphoreType.DMA((3, 3)),
            pltpu.SemaphoreType.DMA((3, 3)),
        ],
        compiler_params=pltpu.CompilerParams(
            collective_id=1, has_side_effects=True, vmem_limit_bytes=VLIM
        ),
        name="feed_forward",
    )(normed_two, ga, w2, wd, resid)


def total(parts):
    acc = parts[0].astype(F32)
    for part in parts[1:]:
        acc = acc + part.astype(F32)
    return acc


def reduce_kernel(
    da_ref, dw_ref, dd_ref,
    oa_ref, og_ref, ou_ref, od_ref,
    ma, sa, mw, sw, md, sd,
    ra1, rb1, ba1, bb1, ra2, rb2, ya, fsib,
    wra1, wrb1, wba1, wbb1, wra2, wrb2, yw,
    dr1, db1, dr2, fin,
    loc, sib_s, sib_r, ss, rs, xs_, xr_,
):
    z, x, y, c = place()
    greet(("z", "x", "y", "c"))
    sibling = peers_of("c")[0]
    off = 64 * (y % 2)

    def cols_of(cc):
        return pl.ds(pl.multiple_of(cc * QKV, LANE), QKV)

    def down_rows(xx, cc):
        return pl.ds(pl.multiple_of(off + DROWS * xx + DHALF * cc, 8), DHALF)

    other = 1 - c
    to_sib = [
        remote(da_ref.at[:, :, :, cols_of(other)], sa, sib_s.at[0], sib_r.at[0], sibling),
        remote(dw_ref.at[other], sw, sib_s.at[1], sib_r.at[1], sibling),
    ] + [
        remote(dd_ref.at[down_rows(xx, other)], sd.at[xx], sib_s.at[2 + xx], sib_r.at[2 + xx], sibling)
        for xx in range(4)
    ]
    start(to_sib)
    local = [
        pltpu.make_async_copy(da_ref.at[:, :, :, cols_of(c)], ma, loc.at[0]),
        pltpu.make_async_copy(dw_ref.at[c], mw, loc.at[1]),
    ] + [
        pltpu.make_async_copy(dd_ref.at[down_rows(xx, c)], md.at[xx], loc.at[2 + xx])
        for xx in range(4)
    ]
    start(local)
    moves = (1, 3, 2)
    a_cols, b_cols = pl.ds(0, 640), pl.ds(640, 512)
    w_cols = (pl.ds(0, 640), pl.ds(640, 640))
    px, pz, py = peers_of("x"), peers_of("z"), peers_of("y")

    def merge(mine, theirs):
        def body(i, carry):
            zz, xx = i // 4, i % 4
            mine[zz, xx] = (mine[zz, xx].astype(F32) + theirs[zz, xx].astype(F32)).astype(BF)
            return carry

        lax.fori_loop(0, 16, body, 0)

    def first_x(mine, cols, dst, j):
        return [
            remote(mine.at[:, (x + m) % 4, :, cols], dst.at[k], ss.at[j, k], rs.at[j, k], px[k])
            for k, m in enumerate(moves)
        ]

    def first_z(mine, cols, dst, j):
        return [
            remote(mine.at[(z + m) % 4, :, :, cols], dst.at[k], ss.at[j, k], rs.at[j, k], pz[k])
            for k, m in enumerate(moves)
        ]

    def second(buf, index, peers, dst, j):
        return [
            remote(buf.at[(index + m) % 4], dst.at[k], ss.at[j, k], rs.at[j, k], peers[k])
            for k, m in enumerate(moves)
        ]

    local[0].wait()
    to_sib[0].wait_recv()
    merge(ma, sa)
    a1 = first_x(ma, a_cols, ra1, 0)
    b1 = first_z(ma, b_cols, rb1, 1)
    start(a1)
    start(b1)
    local[1].wait()
    to_sib[1].wait_recv()
    merge(mw, sw)
    wa1 = first_x(mw, w_cols[0], wra1, 2)
    wb1 = first_z(mw, w_cols[1], wrb1, 3)
    start(wa1)
    start(wb1)
    for xx in range(4):
        local[2 + xx].wait()
        to_sib[2 + xx].wait_recv()

    def merge_down(i, carry):
        md[i] = (md[i].astype(F32) + sd[i].astype(F32)).astype(BF)
        return carry

    lax.fori_loop(0, 4, merge_down, 0)
    d1 = [
        remote(md.at[(x + m) % 4], dr1.at[k], ss.at[4, k], rs.at[4, k], px[k])
        for k, m in enumerate(moves)
    ]
    start(d1)

    def sum_first(mine_of, recv, buf):
        def body(i, carry):
            buf[i] = total([mine_of(i), recv[0, i], recv[1, i], recv[2, i]]).astype(BF)
            return carry

        lax.fori_loop(0, 4, body, 0)

    wait_recv(a1)
    sum_first(lambda i: ma[i, x, :, a_cols], ra1, ba1)
    a2 = second(ba1, z, pz, ra2, 5)
    start(a2)
    wait_recv(b1)
    sum_first(lambda i: ma[z, i, :, b_cols], rb1, bb1)
    b2 = second(bb1, x, px, rb2, 6)
    start(b2)
    wait_recv(wa1)
    sum_first(lambda i: mw[i, x, :, w_cols[0]], wra1, wba1)
    wa2 = second(wba1, z, pz, wra2, 7)
    start(wa2)
    wait_recv(wb1)
    sum_first(lambda i: mw[z, i, :, w_cols[1]], wrb1, wbb1)
    wb2 = second(wbb1, x, px, wrb2, 8)
    start(wb2)
    wait_recv(d1)
    db1[...] = total([md[x], dr1[0], dr1[1], dr1[2]]).astype(BF)
    slot = (z - y + 3) % 4
    dz = remote(
        db1, dr2.at[jnp.minimum(slot, 2)], xs_.at[0], xr_.at[jnp.minimum(slot, 2)], at(y, x, y, c)
    )

    @pl.when(z != y)
    def _():
        dz.start()

    wait_recv(a2)
    ya[y, :, a_cols] = total([ba1[z], ra2[0], ra2[1], ra2[2]]).astype(BF)
    wait_recv(b2)
    ya[y, :, b_cols] = total([bb1[x], rb2[0], rb2[1], rb2[2]]).astype(BF)
    y1 = ring_copies(ya.at[y], ya.at[y], ss.at[9], rs.at[9], "y")
    start(y1)
    wait_recv(wa2)
    yw[c, y, :, w_cols[0]] = total([wba1[z], wra2[0], wra2[1], wra2[2]]).astype(BF)
    wait_recv(wb2)
    yw[c, y, :, w_cols[1]] = total([wbb1[x], wrb2[0], wrb2[1], wrb2[2]]).astype(BF)
    y2 = ring_copies(yw.at[c, y], yw.at[c, y], ss.at[10], rs.at[10], "y")
    start(y2)
    dy = [
        remote(fin.at[c], fin.at[c], xs_.at[1 + k], xr_.at[3], peer) for k, peer in enumerate(py)
    ]

    @pl.when(z == y)
    def _():
        for k in range(3):
            remote(db1, dr2.at[k], xs_.at[0], xr_.at[k], at(y, x, y, c)).wait_recv()
        fin[c] = total([db1[...], dr2[0], dr2[1], dr2[2]]).astype(BF)
        start(dy)

    wait_recv(y1)
    fsib[c] = total([ya[0], ya[1], ya[2], ya[3]])
    fs = remote(fsib.at[c], fsib.at[c], sib_s.at[6], sib_r.at[6], sibling)
    fs.start()
    wait_recv(y2)
    ws = remote(yw.at[c], yw.at[c], sib_s.at[7], sib_r.at[7], sibling)
    ws.start()

    @pl.when(z != y)
    def _():
        dy[0].wait_recv()

    ds_ = remote(fin.at[c], fin.at[c], sib_s.at[8], sib_r.at[8], sibling)
    ds_.start()
    fs.wait_recv()
    oa_ref[:, 0:QKV] = fsib[0]
    oa_ref[:, QKV:PACK] = fsib[1]
    ws.wait_recv()

    def spread(index, out):
        def piece(yy, lo, n):
            return yw[index, yy, :, lo * LANE : (lo + n) * LANE].astype(F32)

        def put(unit, value):
            out[:, unit * LANE : unit * LANE + value.shape[1]] = value

        put(0, piece(0, 0, 9))
        put(9, piece(0, 9, 1) + piece(1, 0, 1))
        put(10, piece(1, 1, 9))
        put(19, piece(2, 0, 9))
        put(28, piece(2, 9, 1) + piece(3, 0, 1))
        put(29, piece(3, 1, 9))

    spread(0, og_ref)
    spread(1, ou_ref)
    ds_.wait_recv()
    od_ref[0:DHALF] = fin[0].astype(F32)
    od_ref[DHALF:DROWS] = fin[1].astype(F32)

    @pl.when(z != y)
    def _():
        dz.wait_send()

    @pl.when(z == y)
    def _():
        wait_send(dy)

    for group in (to_sib, a1, b1, wa1, wb1, d1, a2, b2, wa2, wb2, y1, y2, [fs], [ws], [ds_]):
        wait_send(group)


def reduce_all(da, dw, dd):
    anyspec = pl.BlockSpec(memory_space=pl.ANY)
    vm = pl.BlockSpec(memory_space=pltpu.VMEM)
    v = lambda *shape: pltpu.VMEM(shape, BF)
    return pl.pallas_call(
        reduce_kernel,
        out_shape=(
            jax.ShapeDtypeStruct((SHARD, PACK), F32),
            jax.ShapeDtypeStruct((SHARD, FF), F32),
            jax.ShapeDtypeStruct((SHARD, FF), F32),
            jax.ShapeDtypeStruct((DROWS, D), F32),
        ),
        in_specs=[anyspec] * 3,
        out_specs=(vm,) * 4,
        scratch_shapes=[
            v(4, 4, SHARD, QKV), v(4, 4, SHARD, QKV),
            v(4, 4, SHARD, FFS), v(4, 4, SHARD, FFS),
            v(4, DHALF, D), v(4, DHALF, D),
            v(3, 4, SHARD, 640), v(3, 4, SHARD, 512), v(4, SHARD, 640), v(4, SHARD, 512),
            v(3, SHARD, 640), v(3, SHARD, 512), v(4, SHARD, QKV), pltpu.VMEM((2, SHARD, QKV), F32),
            v(3, 4, SHARD, 640), v(3, 4, SHARD, 640), v(4, SHARD, 640), v(4, SHARD, 640),
            v(3, SHARD, 640), v(3, SHARD, 640), v(2, 4, SHARD, FFS),
            v(3, DHALF, D), v(DHALF, D), v(3, DHALF, D), v(2, DHALF, D),
            pltpu.SemaphoreType.DMA((6,)),
            pltpu.SemaphoreType.DMA((9,)),
            pltpu.SemaphoreType.DMA((9,)),
            pltpu.SemaphoreType.DMA((11, 3)),
            pltpu.SemaphoreType.DMA((11, 3)),
            pltpu.SemaphoreType.DMA((4,)),
            pltpu.SemaphoreType.DMA((4,)),
        ],
        compiler_params=pltpu.CompilerParams(
            collective_id=2, has_side_effects=True, vmem_limit_bytes=VLIM
        ),
        name="reduce_grads",
    )(da, dw, dd)


def rope_tables(positions, head_dim):
    half_dim = head_dim // 2
    exponent = jnp.arange(half_dim, dtype=jnp.float32) * (2.0 / head_dim)
    inverse = ROPE_BASE ** (-exponent)
    angles = positions.astype(jnp.float32)[:, None] * inverse[None, :]
    angles = jnp.concatenate([angles, angles], axis=1)
    return (jnp.cos(angles), jnp.sin(angles))


def rotate_half(inputs, head_dim):
    shaped = inputs.reshape(inputs.shape[:-1] + (inputs.shape[-1] // head_dim, 2, head_dim // 2))
    turned = jnp.stack([-shaped[..., 1, :], shaped[..., 0, :]], axis=-2)
    return turned.reshape(inputs.shape)


def rotate(inputs, cosine, sine, head_dim, direction):
    count = inputs.shape[-1] // head_dim
    cos_all = jnp.tile(cosine, (1, count))
    sin_all = jnp.tile(sine, (1, count))
    return inputs * cos_all + direction * rotate_half(inputs, head_dim) * sin_all


def visible_mask(query_pos, key_pos, start):
    inside_query = (query_pos >= start) & (query_pos < start + PIC)
    inside_key = (key_pos >= start) & (key_pos < start + PIC)
    return (key_pos[None, :] <= query_pos[:, None]) | inside_query[:, None] & inside_key[None, :]


def norm_rows(inputs, gain_row):
    inverse = lax.rsqrt(jnp.mean(inputs * inputs, axis=-1, keepdims=True) + EPSILON)
    return (inverse, inputs * inverse * gain_row)


def norm_back(inputs, inverse, gain_row, grad_normed):
    scaled_in = inputs * inverse
    gain_grad = jnp.sum(grad_normed * scaled_in, axis=0)
    weighted = grad_normed * gain_row
    grad_in = inverse * weighted - scaled_in * inverse * jnp.mean(
        weighted * scaled_in, axis=-1, keepdims=True
    )
    return (grad_in, gain_grad)


def per_device(
    layer_input,
    pic_start,
    norm_one,
    w_query,
    b_query,
    w_key,
    b_key,
    w_value,
    b_value,
    w_out,
    norm_two,
    w_gate,
    w_up,
    w_down,
    out_grad,
):
    micro_count, seq_count, row_count, model_width = layer_input.shape
    length = row_count * lax.axis_size("seq")
    tokens = seq_count * row_count
    tokens2 = micro_count * tokens
    group = HEADS // KV_HEADS
    score_scale = HD ** (-0.5)
    query_pos = lax.axis_index("seq") * row_count + jnp.arange(row_count, dtype=jnp.int32)
    key_pos = jnp.arange(length, dtype=jnp.int32)
    cosine, sine = rope_tables(jnp.tile(query_pos, micro_count * seq_count), HD)

    def scores_of(query_heads, key_heads, start):
        scores = (
            jnp.einsum("rkgd,lkd->kgrl", query_heads, key_heads, preferred_element_type=jnp.float32)
            * score_scale
        )
        return jnp.where(visible_mask(query_pos, key_pos, start), scores, NEGATIVE)

    def attend_forward(element):
        q_seq, k_seq, v_seq, start = element
        query_heads = q_seq.reshape(row_count, KV_HEADS, group, HD)
        key_heads = k_seq.reshape(length, KV_HEADS, HD)
        value_heads = v_seq.reshape(length, KV_HEADS, HD)
        masked = scores_of(query_heads, key_heads, start)
        row_max = jnp.max(masked, axis=-1, keepdims=True)
        unnormed = jnp.exp(masked - row_max)
        row_total = jnp.sum(unnormed, axis=-1, keepdims=True)
        probs = (unnormed / row_total).astype(jnp.bfloat16)
        attended = jnp.einsum(
            "kgrl,lkd->rkgd", probs, value_heads, preferred_element_type=jnp.float32
        )
        return (
            attended.reshape(row_count, HEADS * HD).astype(jnp.bfloat16),
            row_max + jnp.log(row_total),
        )

    def attend_backward(element):
        q_seq, k_seq, v_seq, start, log_total, grad_seq = element
        query_heads = q_seq.reshape(row_count, KV_HEADS, group, HD)
        key_heads = k_seq.reshape(length, KV_HEADS, HD)
        value_heads = v_seq.reshape(length, KV_HEADS, HD)
        grad_heads = grad_seq.reshape(row_count, KV_HEADS, group, HD)
        probs = jnp.exp(scores_of(query_heads, key_heads, start) - log_total)
        rounded = probs.astype(jnp.bfloat16)
        prob_grad = jnp.einsum(
            "rkgd,lkd->kgrl", grad_heads, value_heads, preferred_element_type=jnp.float32
        )
        centre = jnp.sum(probs * prob_grad, axis=-1, keepdims=True)
        score_grad = (probs * (prob_grad - centre)).astype(jnp.bfloat16)
        query_grad = (
            jnp.einsum("kgrl,lkd->rkgd", score_grad, key_heads, preferred_element_type=jnp.float32)
            * score_scale
        )
        key_grad = (
            jnp.einsum(
                "kgrl,rkgd->lkd", score_grad, query_heads, preferred_element_type=jnp.float32
            )
            * score_scale
        )
        value_grad = jnp.einsum(
            "kgrl,rkgd->lkd", rounded, grad_heads, preferred_element_type=jnp.float32
        )
        return (
            query_grad.reshape(row_count, HEADS * HD),
            key_grad.reshape(length, KV_HEADS * HD),
            value_grad.reshape(length, KV_HEADS * HD),
        )


    pad8 = lambda v: jnp.pad(v, (0, SHARD - v.shape[0]))
    ext = jnp.stack([norm_one, norm_two, b_query, pad8(b_key), pad8(b_value)], axis=1)
    ext = jnp.pad(ext, ((0, 0), (0, 256 - 5)))
    pack = jnp.concatenate([w_query, w_key, w_value, w_out, ext], axis=1)
    grads_in = out_grad.reshape(tokens2, D)
    p4, w4, wd, ga = gather_all(pack, w_gate, w_up, w_down, grads_in)
    pf = p4.reshape(D, PACK)
    w2 = w4.reshape(2, D, FFS)
    extf = pf[:, 2048:2056].astype(F32)
    gain_one, gain_two, qbias = extf[:, 0], extf[:, 1], extf[:, 2]
    kbias = extf[:, 3].reshape(16, SHARD)[:, :8].reshape(128)
    vbias = extf[:, 4].reshape(16, SHARD)[:, :8].reshape(128)
    inputs = layer_input.reshape(tokens2, D).astype(F32)
    inv_one, normed_float = norm_rows(inputs, gain_one)
    normed = normed_float.astype(BF)
    qkv = jnp.dot(normed, pf[:, :QKV], preferred_element_type=F32)
    qkv = qkv + jnp.concatenate([qbias, kbias, vbias])
    queries = rotate(qkv[:, :D], cosine, sine, HD, 1.0).astype(BF)
    keys = rotate(qkv[:, D : D + 128], cosine, sine, HD, 1.0).astype(BF)
    values = qkv[:, D + 128 :].astype(BF)
    kv = jnp.concatenate([keys, values], axis=1).reshape(2, row_count, 256)
    kv_all = lax.all_gather(kv, "seq", axis=1, tiled=True)
    keys_all, values_all = kv_all[..., :128], kv_all[..., 128:]
    query_seqs = queries.reshape(2, row_count, D)
    starts = pic_start.reshape(2)
    attended, log_total = lax.map(attend_forward, (query_seqs, keys_all, values_all, starts))
    att_rows = attended.reshape(tokens2, D)
    w_out_full = pf[:, QKV : QKV + D]
    resid = inputs + jnp.dot(att_rows, w_out_full, preferred_element_type=F32)
    inv_two, normed_two_float = norm_rows(resid, gain_two)
    normed_two = normed_two_float.astype(BF)
    output, grad_normed_two, dw, dd = feed_forward(normed_two, ga, w2, wd, resid)
    grad_middle, gain_two_grad = norm_back(resid, inv_two, gain_two, grad_normed_two)
    resid_grad = grads_in.astype(F32) + grad_middle
    attn_grad_low = resid_grad.astype(BF)
    out_wgrad = outer_sum(att_rows, attn_grad_low)
    heads_grad = back_dot(attn_grad_low, w_out_full).astype(BF)
    query_grad, key_part, value_part = lax.map(
        attend_backward,
        (query_seqs, keys_all, values_all, starts, log_total, heads_grad.reshape(2, row_count, D)),
    )
    kv_part = jnp.concatenate([key_part, value_part], axis=2).astype(BF)
    kv_grad = lax.psum_scatter(kv_part, "seq", scatter_dimension=1, tiled=True)
    kv_grad = kv_grad.astype(F32).reshape(tokens2, 256)
    qlin_grad = rotate(query_grad.reshape(tokens2, D), cosine, sine, HD, -1.0).astype(BF)
    klin_grad = rotate(kv_grad[:, :128], cosine, sine, HD, -1.0).astype(BF)
    vlin_grad = kv_grad[:, 128:].astype(BF)
    lin_grad = jnp.concatenate([qlin_grad, klin_grad, vlin_grad], axis=1)
    grad_normed = back_dot(lin_grad, pf[:, :QKV])
    grad_first, gain_one_grad = norm_back(inputs, inv_one, gain_one, grad_normed)
    input_grad = (resid_grad + grad_first).reshape(micro_count, seq_count, row_count, D)
    qkv_wgrad = outer_sum(normed, lin_grad)
    bias_grad = jnp.sum(lin_grad.astype(F32), axis=0)
    spread = lambda v: jnp.pad(v.reshape(16, 8), ((0, 0), (0, SHARD - 8))).reshape(D)
    ext_grad = jnp.stack(
        [gain_one_grad, gain_two_grad, bias_grad[:D], spread(bias_grad[D : D + 128]), spread(bias_grad[D + 128 :])],
        axis=1,
    )
    ext_grad = jnp.pad(ext_grad, ((0, 0), (0, 256 - 5)))
    da = jnp.concatenate([qkv_wgrad, out_wgrad, ext_grad], axis=1).astype(BF)
    oa, og, ou, od = reduce_all(
        da.reshape(4, 4, SHARD, PACK), dw.reshape(2, 4, 4, SHARD, FFS), dd
    )
    return (
        output.reshape(micro_count, seq_count, row_count, D),
        input_grad,
        oa[:, 2048],
        oa[:, :D],
        oa[:, 2050],
        oa[:, D : D + 128],
        oa[:8, 2051],
        oa[:, D + 128 : QKV],
        oa[:8, 2052],
        oa[:, QKV : QKV + D],
        oa[:, 2049],
        og,
        ou,
        od,
    )


def solution(mesh):
    placed = (
        P(None, "dp", "seq", None),
        P(None, "dp"),
        P("dp"),
        P("dp", None),
        P("dp"),
        P("dp", None),
        P("dp"),
        P("dp", None),
        P("dp"),
        P("dp", None),
        P("dp"),
        P("dp", None),
        P("dp", None),
        P("dp", None),
        P(None, "dp", "seq", None),
    )
    return jax.shard_map(
        per_device,
        mesh=mesh,
        in_specs=placed,
        out_specs=(
            P(None, "dp", "seq", None),
            P(None, "dp", "seq", None),
            P("dp"),
            P("dp", None),
            P("dp"),
            P("dp", None),
            P("dp"),
            P("dp", None),
            P("dp"),
            P("dp", None),
            P("dp"),
            P("dp", None),
            P("dp", None),
            P("dp", None),
        ),
        check_vma=False,
    )
```

time: 1250 us -> 410 us (0.33)
  waiting for transfers between devices: 750 us -> 36.8 us
  Pallas kernels: 0 us -> 220 us
  blocking collectives: 218 us -> 0 us
  matrix products: 164 us -> 47.4 us
  other arithmetic: 48.1 us -> 33.3 us
    unnamed x28 -> x3, waiting for transfers between devices: 595 us -> 16.8 us
    pallas_call x0 -> x3, Pallas kernels: none -> 220 us  [the longest x1 78.2 us: reduce_all(): pl.pallas_call(reduce_kernel, out_shape=(jax.ShapeDtypeStruct((SHARD, PAC...]
    dot_general x42 -> x6, matrix products: 125 us -> 16.2 us  [the longest x2 6.58 us: back_dot(): jnp.einsum('tb,ab->ta', grad_rows, weight, preferred_element_type=F32)]
    all_gather x6 -> x0, blocking collectives: 102 us -> none  [the longest x2 37.4 us: per_device(): lax.all_gather(values.reshape(seq_count, row_count, KV_HEADS * HD), 'seq'...]
    all_gather x5 -> x1, waiting for transfers between devices: 116 us -> 20 us  [per_device(): kv_all = lax.all_gather(kv, 'seq', axis=1, tiled=True)]
    unnamed x2 -> x0, blocking collectives: 93.9 us -> none
    psum x1 -> x0, waiting for transfers between devices: 40.2 us -> none  [per_device(): lax.psum(shares[1].astype(jnp.bfloat16), 'seq').astype(jnp.float32)]
    psum x1 -> x0, blocking collectives: 21.7 us -> none  [per_device(): lax.psum(shares[0].astype(jnp.bfloat16), 'seq').astype(jnp.float32)]
  transfers between devices with their start and end apart: 17 -> 2, of which waited for: 11 -> 2; matrix products, arithmetic and copies ran while one was open for 15% -> 5% of each run, Pallas kernels for 0% -> 0%
where the time goes in v1:
time: 410 us; the launch traced here: 404 us
  Pallas kernels  220 us (54%)
  local copies, waits for them, and re-layouts  47.7 us (12%)
  matrix products  47.4 us (12%)
  waiting for transfers between devices  36.8 us (9%)
  other arithmetic  33.3 us (8%)
  between operations  14.9 us (4%)
    pallas_call x1, Pallas kernels, reduce_all(): pl.pallas_call(reduce_kernel, out_shape=(jax.ShapeDtypeStruct((SHARD, PAC...  78.2 us
    pallas_call x1, Pallas kernels, gather_all(): pl.pallas_call(gather_kernel, out_shape=(jax.ShapeDtypeStruct((4, 4, SHAR...  72 us
    pallas_call x1, Pallas kernels, feed_forward(): pl.pallas_call(mlp_kernel, out_shape=(jax.ShapeDtypeStruct((ROWS, D), BF)...  70.1 us
    all_gather x1, waiting for transfers between devices, per_device(): kv_all = lax.all_gather(kv, 'seq', axis=1, tiled=True)  20 us
    unnamed x3, waiting for transfers between devices  16.8 us
    unnamed x70, local copies, waits for them, and re-layouts  13.1 us
    dot_general x4, matrix products, scores_of(): jnp.einsum('rkgd,lkd->kgrl', query_heads, key_heads, preferred_element_ty...  10.6 us
    dot_general x2, matrix products, attend_backward(): jnp.einsum('rkgd,lkd->kgrl', grad_heads, value_heads, preferred_element_t...  8.96 us
  transfers between devices with their start and end apart: 2, of which 2 were waited for; matrix products, arithmetic and copies ran while one was open for 5% of the time, Pallas kernels for 0%

profile of v1, /device:TPU:9, one launch (start us, length us, event | category | flops | bytes accessed | tf_op | source)
XLA Modules:
  0.0 403.9 jit_solution(11724821636089664316)
XLA Ops:
  12.8 72.0 %gather_weights.1 = (bf16[4,4,56,2304]{3,2,1,0:T(8,128)(2,1)}, bf16[2,4,4,56,1280]{4,3,2,1,0:T(8,128)(2,1)}, bf16[1280,896]{1,0:T(8,128)(2,1)}, bf16[4,256,896]{2,1,0:T(8,128)(2,1)}) custom-call(bf16[56,2304]{1,0:T(8,128)(2,1)} %copy-done.25, bf16[56,4864]{1,0:T(8,128)(2,1)} %wg_ref.1, bf16[56,4864]{1,0:T(8,128)(2,1)} %wu_ref.1, bf16[304,896]{1,0:T(8,128)(2,1)} %wd_ref.1, ...), custom_call_target="tpu_custom_call" | custom-call | tf_op jit(solution)/shard_map/gather_weights/pallas_call | solution.py:219
  89.0 2.4 convolution_add_fusion
  97.2 2.0 add_convert_fusion
  99.5 20.0 %all-gather.2.cloned.1.call-done = bf16[2,1024,256]{1,2,0:T(8,128)(2,1)} async-done(((bf16[2,128,256]{1,2,0:T(8,128)(2,1)}), bf16[2,1024,256]{1,2,0:T(8,128)(2,1)}) %all-gather.2.cloned.1.call-update) | async-done | bytes 1048592 | tf_op jit(solution)/shard_map/all_gather | solution.py:788
  120.7 17.3 %while.30 = (s32[]{:T(128)}, bf16[2,128,896]{2,1,0:T(8,128)(2,1)}, f32[2,2,7,128,1]{3,2,1,4,0:T(8,128)S(1)}, bf16[2,1024,128]{1,2,0:T(8,128)(2,1)S(1)}, s32[2]{0...) while((s32[]{:T(128)}, bf16[2,128,896]{2,1,0:T(8,128)(2,1)}, ...), condition=%wide.region_4.5_spmd.clone.clone, body=%wide.region_1.4_spmd.clone.clone.sunk | while | flops 492291968 | bytes 29686236 | solution.py:792
  126.5 2.0 fusion.105
  135.1 2.0 fusion.105
  138.1 2.4 multiply_reduce_fusion.4
  141.5 70.1 %feed_forward.1 = (bf16[256,896]{1,0:T(8,128)(2,1)}, f32[256,896]{1,0:T(8,128)}, bf16[2,896,1280]{2,1,0:T(8,128)(2,1)}, bf16[1280,896]{1,0:T(8,128)(2,1)}) custom-call(bf16[256,896]{1,0:T(8,128)(2,1)} %multiply_convert_fusion.x_ref, bf16[4,256,896]{2,1,0:T(8,128)(2,1)} %get-tuple-element.152.ga_ref, bf16[2,896,1280]{2,1,0:T(8,128)(2,1)} %bitcast.267, ...), custom_call_target="tpu_custom_call" | custom-call | tf_op jit(solution)/shard_map/feed_forward/pallas_call | solution.py:358
  211.7 1.8 multiply_reduce_fusion
  213.5 1.8 subtract_add_fusion.1
  215.3 2.9 fusion.40
  218.2 39.2 %while.31 = (s32[]{:T(128)}, f32[2,128,896]{1,2,0:T(8,128)}, bf16[2,1024,128]{1,2,0:T(8,128)(2,1)}, bf16[2,1024,128]{1,2,0:T(8,128)(2,1)}, bf16[2,1024,128]{1,2,...) while((s32[]{:T(128)}, f32[2,128,896]{1,2,0:T(8,128)}, ...), condition=%wide.region_9.10_spmd.clone.clone, body=%wide.region_7.9_spmd.clone.clone.sunk | while | flops 1202702208 | bytes 94950536 | solution.py:804
  221.0 4.1 %fusion.116 = f32[2,1024,128,7]{2,1,3,0:T(8,128)} fusion(bf16[1024,2,64,1]{0,2,3,1:T(8,128)(2,1)S(1)} %bitcast.253, bf16[128,2,7,64]{0,3,2,1:T(8,128)(2,1)S(1)} %bitcast.255), kind=kOutput, calls=%fused_computation.137.clone.1 | convolution fusion | flops 234881024 | bytes 7831552 | tf_op jit(solution)/shard_map/while/body/eval_jaxpr/rkgd,lkd->kgrl/dot_general | solution.py:711
  225.4 4.5 %fusion.119 = (f32[2,7,128]{2,1,0:T(8,128)S(1)}, f32[2,1024,128,7]{2,1,3,0:T(8,128)S(1)}) fusion(f32[2,1024,128,7]{2,1,3,0:T(8,128)} %fusion.116, f32[2,7,128]{2,1,0:T(8,128)S(1)} %dynamic-slice_bitcast_fusion.2, pred[128,1024]{0,1:T(8,128)(4,1)S(1)} %fusion.118, bf16[1024,2,64,1]{0,2,3,1:T(8,128)(2,1)S(1)} %bitcast.258, ...), kind=kOutput, calls=%fused_computation.27.clone.1 | convolution fusion | flops 244054272 | bytes 15316992 | tf_op jit(solution)/shard_map/while/body/eval_jaxpr/rkgd,lkd->kgrl/dot_general | solution.py:742
  230.7 2.1 fusion.120
  234.1 1.8 fusion.121
  240.7 4.1 %fusion.116 = f32[2,1024,128,7]{2,1,3,0:T(8,128)} fusion(bf16[1024,2,64,1]{0,2,3,1:T(8,128)(2,1)S(1)} %bitcast.253, bf16[128,2,7,64]{0,3,2,1:T(8,128)(2,1)S(1)} %bitcast.255), kind=kOutput, calls=%fused_computation.137.clone.1 | convolution fusion | flops 234881024 | bytes 7831552 | tf_op jit(solution)/shard_map/while/body/eval_jaxpr/rkgd,lkd->kgrl/dot_general | solution.py:711
  245.0 4.5 %fusion.119 = (f32[2,7,128]{2,1,0:T(8,128)S(1)}, f32[2,1024,128,7]{2,1,3,0:T(8,128)S(1)}) fusion(f32[2,1024,128,7]{2,1,3,0:T(8,128)} %fusion.116, f32[2,7,128]{2,1,0:T(8,128)S(1)} %dynamic-slice_bitcast_fusion.2, pred[128,1024]{0,1:T(8,128)(4,1)S(1)} %fusion.118, bf16[1024,2,64,1]{0,2,3,1:T(8,128)(2,1)S(1)} %bitcast.258, ...), kind=kOutput, calls=%fused_computation.27.clone.1 | convolution fusion | flops 244054272 | bytes 15316992 | tf_op jit(solution)/shard_map/while/body/eval_jaxpr/rkgd,lkd->kgrl/dot_general | solution.py:742
  250.3 2.1 fusion.120
  253.7 1.8 fusion.121
  262.2 1.9 copy.146
  264.1 2.4 copy.144
  268.3 2.4 copy.147
  272.0 1.8 convolution_convert_fusion.1
  273.8 2.5 fusion.44
  276.3 16.8 %reduce-scatter.4.cloned.1.call-done = bf16[128,512]{1,0:T(8,128)(2,1)} async-done(((bf16[1024,512]{1,0:T(8,128)(2,1)}), bf16[128,512]{1,0:T(8,128)(2,1)}) %reduce-scatter.4.cloned.1.call-update) | async-done | bytes 131088
  296.6 3.7 multiply_reduce_fusion.1
  300.2 3.1 convolution_convert_fusion
  304.1 3.3 pad_maximum_fusion.da_ref
  307.4 78.2 %reduce_grads.1 = (f32[56,2304]{1,0:T(8,128)}, f32[56,4864]{1,0:T(8,128)}, f32[56,4864]{1,0:T(8,128)}, f32[304,896]{1,0:T(8,128)}) custom-call(bf16[4,4,56,2304]{3,2,1,0:T(8,128)(2,1)} %pad_maximum_fusion.da_ref, bf16[2,4,4,56,1280]{4,3,2,1,0:T(8,128)(2,1)} %bitcast.268, bf16[1280,896]{1,0:T(8,128)(2,1)} %get-tuple-element.162.dd_ref), custom_call_target="tpu_custom_call" | custom-call | tf_op jit(solution)/shard_map/reduce_grads/pallas_call | solution.py:605
  385.7 1.9 fusion.53
  (249 shorter events, 63.4 us)
Async XLA Ops:
  7.2 80.9 %copy-start.6 = (bf16[2,1,128,896]{3,2,1,0:T(8,128)(2,1)S(1)}, bf16[2,1,128,896]{3,2,1,0:T(8,128)(2,1)}, u32[]{:S(2)}) copy-start(bf16[2,1,128,896]{3,2,1,0:T(8,128)(2,1)} %param.19) | copy-start | bytes 1376260
  7.2 112.2 %all-gather.2.cloned.1.call-start = ((), (), s32[]{:S(2)}) async-start(), calls=%async_computation.1 | async-start | bytes 1179648 | tf_op jit(solution)/shard_map/all_gather | solution.py:788
  91.4 2.8 copy-start.8
  93.7 199.4 %reduce-scatter.4.cloned.1.call-start = ((), (), s32[]{:S(2)}) async-start(), calls=%async_computation.2 | async-start | bytes 1179648
  96.8 23.9 %copy-start.1 = (f32[256,896]{1,0:T(8,128)}, f32[256,896]{1,0:T(8,128)S(1)}, u32[]{:S(2)}) copy-start(f32[256,896]{1,0:T(8,128)S(1)} %copy.136) | copy-start | bytes 2752516
  96.9 23.8 %copy-start.34 = (s32[2,1]{0,1:T(1,128)S(1)}, s32[2,1]{0,1:T(1,128)}, u32[]{:S(2)}) copy-start(s32[2,1]{0,1:T(1,128)} %param.20) | copy-start | bytes 28
  97.2 2.2 copy-start.3
  120.7 19.7 %copy-start.29 = (f32[896]{0:T(1024)S(1)}, f32[896]{0:T(1024)}, u32[]{:S(2)}) copy-start(f32[896]{0:T(1024)} %get-tuple-element.406) | copy-start | bytes 10756
  126.5 2.2 copy-start.27
  135.1 2.2 copy-start.27
  141.5 72.0 %copy-start.12 = (bf16[2,1,128,896]{3,2,1,0:T(8,128)(2,1)S(1)}, bf16[2,1,128,896]{3,2,1,0:T(8,128)(2,1)}, u32[]{:S(2)}) copy-start(bf16[2,1,128,896]{3,2,1,0:T(8,128)(2,1)} %param.33) | copy-start | bytes 1376260
  221.0 4.2 %copy-start.9 = (bf16[2,128,896]{2,1,0:T(8,128)(2,1)S(1)}, bf16[2,128,896]{2,1,0:T(8,128)(2,1)}, u32[]{:S(2)}) copy-start(bf16[2,128,896]{2,1,0:T(8,128)(2,1)} %get-tuple-element.679) | copy-start | bytes 1376260 | tf_op jit(solution)/shard_map/while
  225.4 4.5 %slice-start = ((s8[7340032]{0:T(1024)(128)(4,1)}), s8[4194304]{0:T(1024)(128)(4,1)S(1)}, s32[]{:S(2)}) async-start(s8[7340032]{0:T(1024)(128)(4,1)} %bitcast.251), calls=%async_computation.3 | async-start | bytes 8388608 | tf_op jit(solution)/shard_map/while
  225.4 5.3 %slice-start.1 = ((s8[7340032]{0:T(1024)(128)(4,1)}), s8[3145728]{0:T(1024)(128)(4,1)S(1)}, s32[]{:S(2)}) async-start(s8[7340032]{0:T(1024)(128)(4,1)} %bitcast.251), calls=%async_computation.4 | async-start | bytes 6291456 | tf_op jit(solution)/shard_map/while
  234.1 1.8 copy-start.21
  240.6 4.2 %copy-start.9 = (bf16[2,128,896]{2,1,0:T(8,128)(2,1)S(1)}, bf16[2,128,896]{2,1,0:T(8,128)(2,1)}, u32[]{:S(2)}) copy-start(bf16[2,128,896]{2,1,0:T(8,128)(2,1)} %get-tuple-element.679) | copy-start | bytes 1376260 | tf_op jit(solution)/shard_map/while
  245.0 4.5 %slice-start = ((s8[7340032]{0:T(1024)(128)(4,1)}), s8[4194304]{0:T(1024)(128)(4,1)S(1)}, s32[]{:S(2)}) async-start(s8[7340032]{0:T(1024)(128)(4,1)} %bitcast.251), calls=%async_computation.3 | async-start | bytes 8388608 | tf_op jit(solution)/shard_map/while
  245.0 5.3 %slice-start.1 = ((s8[7340032]{0:T(1024)(128)(4,1)}), s8[3145728]{0:T(1024)(128)(4,1)S(1)}, s32[]{:S(2)}) async-start(s8[7340032]{0:T(1024)(128)(4,1)} %bitcast.251), calls=%async_computation.4 | async-start | bytes 6291456 | tf_op jit(solution)/shard_map/while
  253.7 1.8 copy-start.21
  257.4 3.8 copy-start.11
  267.3 6.5 %copy-start.2 = (f32[256,896]{1,0:T(8,128)S(1)}, f32[256,896]{1,0:T(8,128)}, u32[]{:S(2)}) copy-start(f32[256,896]{1,0:T(8,128)} %copy-done.1) | copy-start | bytes 2752516
  267.3 6.5 %copy-start.4 = (f32[256,896]{1,0:T(8,128)S(1)}, f32[256,896]{1,0:T(8,128)}, u32[]{:S(2)}) copy-start(f32[256,896]{1,0:T(8,128)} %copy-done.3) | copy-start | bytes 2752516
  273.8 22.7 %copy-start.7 = (bf16[2,1,128,896]{3,2,1,0:T(8,128)(2,1)S(1)}, bf16[2,1,128,896]{3,2,1,0:T(8,128)(2,1)}, u32[]{:S(2)}) copy-start(bf16[2,1,128,896]{3,2,1,0:T(8,128)(2,1)} %param.19) | copy-start | bytes 1376260
  273.8 22.7 %copy-start.31 = (f32[896]{0:T(1024)S(1)}, f32[896]{0:T(1024)}, u32[]{:S(2)}) copy-start(f32[896]{0:T(1024)} %copy-done.30) | copy-start | bytes 10756
  273.8 22.7 %copy-start.33 = (f32[256]{0:T(256)S(1)}, f32[256]{0:T(256)}, u32[]{:S(2)}) copy-start(f32[256]{0:T(256)} %copy-done.32) | copy-start | bytes 3076
  294.2 6.0 %copy-start.13 = (bf16[256,896]{1,0:T(8,128)(2,1)S(1)}, bf16[256,896]{1,0:T(8,128)(2,1)}, u32[]{:S(2)}) copy-start(bf16[256,896]{1,0:T(8,128)(2,1)} %fusion.44) | copy-start | bytes 1376260
  296.5 7.6 %copy-start.5 = (bf16[4,4,56,896]{3,2,1,0:T(8,128)(2,1)S(1)}, bf16[4,4,56,896]{3,2,1,0:T(8,128)(2,1)}, u32[]{:S(2)}) copy-start(bf16[4,4,56,896]{3,2,1,0:T(8,128)(2,1)} %convolution_convert_fusion.1) | copy-start | bytes 4816900
  307.4 84.7 %copy-start.19 = (f32[256,896]{1,0:T(8,128)S(1)}, f32[256,896]{1,0:T(8,128)}, u32[]{:S(2)}) copy-start(f32[256,896]{1,0:T(8,128)} %get-tuple-element.479) | copy-start | bytes 2752516
  385.6 7.7 %copy-start.26 = (bf16[256,896]{1,0:T(8,128)(2,1)S(1)}, bf16[256,896]{1,0:T(8,128)(2,1)}, u32[]{:S(2)}) copy-start(bf16[256,896]{1,0:T(8,128)(2,1)} %get-tuple-element.155) | copy-start | bytes 1376260
  385.6 8.4 %copy-start.18 = (f32[56,4864]{1,0:T(8,128)S(1)}, f32[56,4864]{1,0:T(8,128)}, u32[]{:S(2)}) copy-start(f32[56,4864]{1,0:T(8,128)} %get-tuple-element.708) | copy-start | bytes 3268612
  385.7 9.4 %copy-start.17 = (f32[56,4864]{1,0:T(8,128)S(1)}, f32[56,4864]{1,0:T(8,128)}, u32[]{:S(2)}) copy-start(f32[56,4864]{1,0:T(8,128)} %get-tuple-element.709) | copy-start | bytes 3268612
  392.1 4.0 copy-start.16
  (16 other events, 16.2 us)
Sparse Core Ops, SparseCore 0:
  93.8 25.6 all-gather.1
  261.3 31.7 reduce-scatter.3
